TPU v7x, 32 devices: a whole 2x2x4 slice. The times are simulated.
32 devices in a mesh: occ: 4 (over y, x), vir: 8 (over z, core).
Axes of the slice: x: 2, y: 2, z: 4, core: 2. Of those that a mesh axis runs over, the one named last changes fastest.
Arguments:
- amplitudes: bfloat16 [2048, 16384], P('occ', 'vir'), may hold values from -6 to 6
- integrals: bfloat16 [16384, 512], P('vir', 'occ'), may hold values from -0.09375 to 0.09375
- active: int32 [16, 128], P('occ', 'vir'), may hold values from 0 to 1
Outputs:
- residual: bfloat16 [2048, 512], P('occ', 'vir')
All inputs are finite; a program needn't handle non-finite values.
Results may differ from a plain program's by a relative error of at most 0.001.
Values may be sent and summed in bfloat16 or wider, within the bound.
A program may use at most 64 MiB of HBM per device.

v0:
```python
import functools
import math

import jax
import jax.numpy as jnp
from jax import lax
from jax.experimental import pallas as pl
from jax.experimental.pallas import tpu as pltpu
from jax.sharding import PartitionSpec as P

TILE = 128
CHUNKS = 4
MESH = pl.DeviceIdType.MESH


def fast_side(count):
    side = math.isqrt(count)
    while count % side:
        side -= 1
    return side


def kernel(
    p, q, nz, active, a_hbm, b_hbm, out, a, raw, b, part, got, zsend, zrecv,
    a_sem, b_sem, own_sem, fwd_sem, recv_sem, give_sem, got_sem, zsend_sem, zrecv_sem, reach_sem,
):
    o = lax.axis_index("occ")
    v = lax.axis_index("vir")
    core, z = lax.rem(v, 2), lax.div(v, 2)
    pi, qi = lax.div(o, q), lax.rem(o, q)
    rows, depth = a.shape
    width = raw.shape[1]
    sub = width // CHUNKS
    deep = depth // CHUNKS
    tall = rows // CHUNKS
    short = tall // 2
    per_core = CHUNKS // 2
    halves = (pl.ds(0, deep // 2), pl.ds(deep // 2, deep // 2))
    sibling = (o, v + 1 - 2 * core)
    below, above = (o, v - 2), (o, v + 2)
    f32 = jnp.float32

    def occ_at(dp, dq):
        return lax.rem(pi + dp, p) * q + lax.rem(qi + dq, q)

    def slot(dp, dq):
        return (dp % p) * q + dq % q

    def signal(sem, peer):
        pl.semaphore_signal(sem, inc=1, device_id=peer, device_id_type=MESH)

    b_copy = pltpu.make_async_copy(b_hbm, raw, b_sem)
    b_copy.start()
    a_copy = pltpu.make_async_copy(a_hbm, a, a_sem)
    a_copy.start()

    barrier = pltpu.get_barrier_semaphore()
    near = [sibling]
    near += [(occ_at(0, d), v) for d in range(1, q)]
    near += [(occ_at(d, 0), v) for d in range(1, p)]
    for peer in near:
        signal(barrier, peer)
    pl.when(z > 0)(lambda: signal(barrier, below))
    pl.when(z < nz - 1)(lambda: signal(barrier, above))

    def group_of(shape):
        return lax.div(lax.broadcasted_iota(jnp.int32, shape, 1), sub)

    b_copy.wait()
    group = group_of((deep, width))
    quarters = [raw[k * deep : (k + 1) * deep].astype(f32) for k in range(CHUNKS)]
    for j in range(CHUNKS):
        packed = None
        for k in range(CHUNKS):
            turn = (sub * (k - j)) % width
            piece = pltpu.roll(quarters[k], turn, 1) if turn else quarters[k]
            packed = piece if packed is None else jnp.where(group == k, piece, packed)
        b[0, j] = packed.astype(b.dtype)

    beside = lax.div(z + nz - 1, nz) + lax.div(2 * nz - 2 - z, nz)
    pl.semaphore_wait(barrier, len(near) + beside)

    sends = []

    def remote(src, dst, send_sem, to_sem, peer):
        copy = pltpu.make_async_remote_copy(
            src_ref=src, dst_ref=dst, send_sem=send_sem, recv_sem=to_sem,
            device_id=peer, device_id_type=MESH,
        )
        copy.start()
        return copy

    def send_own(j, stage):
        if j >= CHUNKS:
            return
        moves = [(0, d, stage) for d in range(1, q)] + [(d, 0, 1 - stage) for d in range(1, p)]
        for dp, dq, h in moves:
            s = slot(-dp, -dq)
            sends.append(
                remote(
                    b.at[0, j, halves[h]], b.at[s, j, halves[h]],
                    own_sem.at[s, j, h], recv_sem.at[s, j, h], (occ_at(dp, dq), v),
                )
            )

    def forward(sp, sq, dp, dq, j, h):
        s, t = slot(sp, sq), slot(sp - dp, sq - dq)
        sends.append(
            remote(
                b.at[s, j, halves[h]], b.at[t, j, halves[h]],
                fwd_sem.at[t, j, h], recv_sem.at[t, j, h], (occ_at(dp, dq), v),
            )
        )

    def arrived(dp, dq, j, h):
        s = slot(dp, dq)
        place = b.at[s, j, halves[h]]
        pltpu.make_async_copy(place, place, recv_sem.at[s, j, h]).wait()

    def reach(step):
        pl.when(z > 0)(lambda: signal(reach_sem.at[step, 1], below))
        pl.when(z < nz - 1)(lambda: signal(reach_sem.at[step, 0], above))

    def reached(step):
        pl.when(z > 0)(lambda: pl.semaphore_wait(reach_sem.at[step, 0], 1))
        pl.when(z < nz - 1)(lambda: pl.semaphore_wait(reach_sem.at[step, 1], 1))

    send_own(0, 0)
    send_own(0, 1)
    send_own(1, 0)
    reach(0)

    a_copy.wait()
    for r in range(rows // TILE):
        for e in range(depth // TILE):
            place = (pl.ds(r * TILE, TILE), pl.ds(e * TILE, TILE))
            weight = active[r, e].astype(f32)
            a[place] = (a[place].astype(f32) * weight).astype(a.dtype)

    for step in range(1, nz - 1):
        reached(step - 1)
        reach(step)
    lanes = group_of((tall, width))

    def multiply(dp, dq, j):
        s = slot(dp, dq)
        block = b[s, j]
        parts = [
            jnp.dot(a[:, k * deep : (k + 1) * deep], block, preferred_element_type=f32)
            for k in range(CHUNKS)
        ]
        summed = None
        for d in range(CHUNKS):
            mixed = None
            for k in range(CHUNKS):
                r = (k + d) % CHUNKS
                piece = parts[k][r * tall : (r + 1) * tall]
                mixed = piece if mixed is None else jnp.where(lanes == k, piece, mixed)
            mixed = pltpu.roll(mixed, sub * d, 1) if d else mixed
            summed = mixed if summed is None else summed + mixed
        part[s, j, 0] = summed[:short]
        part[s, j, 1] = summed[short:]
        copy = remote(
            part.at[s, j, 1 - core], got.at[s, j], give_sem.at[s, j], got_sem.at[s, j], sibling
        )
        return dp, dq, j, copy

    def z_copy(dp, dq, j):
        s = slot(dp, dq)
        owner = occ_at(dp, dq)
        place = lax.rem(z - owner + nz, nz)
        keeper = j // per_core
        return pltpu.make_async_remote_copy(
            src_ref=zsend.at[s, j],
            dst_ref=zrecv.at[j % per_core, place, core],
            send_sem=zsend_sem.at[s, j],
            recv_sem=zrecv_sem.at[j % per_core, place, core],
            device_id=(o, owner * 2 + keeper),
            device_id_type=MESH,
        )

    def stays(dp, dq, j):
        return occ_at(dp, dq) * 2 + j // per_core == v

    def hand_over(dp, dq, j, copy):
        s = slot(dp, dq)
        copy.wait()
        value = part[s, j, core] + got[s, j]

        @pl.when(stays(dp, dq, j))
        def _():
            zrecv[j % per_core, 0, core] = value

        @pl.when(jnp.logical_not(stays(dp, dq, j)))
        def _():
            zsend[s, j] = value
            z_copy(dp, dq, j).start()

    pending = []

    def run(dp, dq, j):
        pending.append(multiply(dp, dq, j))
        while len(pending) > 1:
            hand_over(*pending.pop(0))

    def diagonals(j):
        for dp in range(1, p):
            for dq in range(1, q):
                arrived(dp, dq, j, 0)
                arrived(dp, dq, j, 1)
                run(dp, dq, j)

    first = multiply(0, 0, 0)
    pending.append(first)
    reached(nz - 2)
    for j in range(CHUNKS):
        for d in range(1, q):
            arrived(0, d, j, 0)
            for f in range(1, p):
                forward(0, d, f, 0, j, 0)
        for d in range(1, p):
            arrived(d, 0, j, 1)
            for f in range(1, q):
                forward(d, 0, 0, f, j, 1)
        send_own(j + 1, 1)
        send_own(j + 2, 0)
        if j:
            diagonals(j - 1)
        if j + 1 < CHUNKS:
            run(0, 0, j + 1)
        for d in range(1, q):
            arrived(0, d, j, 1)
            run(0, d, j)
        for d in range(1, p):
            arrived(d, 0, j, 0)
            run(d, 0, j)
    while pending:
        hand_over(*pending.pop(0))
    diagonals(CHUNKS - 1)
    while pending:
        hand_over(*pending.pop(0))

    sums = {}
    for g in range(per_core):
        for k in range(2):
            for d in range(nz):

                def wait(g=g, d=d, k=k):
                    place = zrecv.at[g, d, k]
                    pltpu.make_async_copy(place, place, zrecv_sem.at[g, d, k]).wait()

                if d:
                    wait()
                else:
                    pl.when(core != k)(wait)
            total = zrecv[g, 0, k]
            for d in range(1, nz):
                total = total + zrecv[g, d, k]
            sums[g, k] = total
    small = group_of((short, width))
    for r in range(CHUNKS):
        for k in range(2):
            value = None
            for g in range(per_core):
                turn = (sub * (g - r)) % width
                piece = pltpu.roll(sums[g, k], turn, 1) if turn else sums[g, k]
                value = piece if value is None else jnp.where(small == g, piece, value)
            start = r * tall + k * short
            out[start : start + short] = value[:, : width // 2].astype(out.dtype)

    for copy in sends:
        copy.wait_send()
    for j in range(CHUNKS):
        for dp in range(p):
            for dq in range(q):

                @pl.when(jnp.logical_not(stays(dp, dq, j)))
                def _():
                    z_copy(dp, dq, j).wait_send()


def on_device(nocc, nvir, amplitudes, integrals, active):
    rows, depth = amplitudes.shape
    width = integrals.shape[1]
    q = fast_side(nocc)
    p = nocc // q
    nz = nvir // 2
    g = CHUNKS
    short = rows // g // 2
    f32 = jnp.float32
    any_space = pl.BlockSpec(memory_space=pl.ANY)
    dma = pltpu.SemaphoreType.DMA
    return pl.pallas_call(
        functools.partial(kernel, p, q, nz),
        out_shape=jax.ShapeDtypeStruct((rows, width // 2), jnp.bfloat16),
        in_specs=[pl.BlockSpec(memory_space=pltpu.SMEM), any_space, any_space],
        out_specs=pl.BlockSpec(memory_space=pltpu.VMEM),
        scratch_shapes=[
            pltpu.VMEM((rows, depth), amplitudes.dtype),
            pltpu.VMEM((depth, width), integrals.dtype),
            pltpu.VMEM((nocc, g, depth // g, width), integrals.dtype),
            pltpu.VMEM((nocc, g, 2, short, width), f32),
            pltpu.VMEM((nocc, g, short, width), f32),
            pltpu.VMEM((nocc, g, short, width), f32),
            pltpu.VMEM((g // 2, nz, 2, short, width), f32),
            dma(()), dma(()),
            dma((nocc, g, 2)), dma((nocc, g, 2)), dma((nocc, g, 2)),
            dma((nocc, g)), dma((nocc, g)), dma((nocc, g)), dma((g // 2, nz, 2)),
            pltpu.SemaphoreType.REGULAR((nz - 1, 2)),
        ],
        compiler_params=pltpu.CompilerParams(collective_id=0, has_side_effects=True),
    )(active, amplitudes, integrals)


def solution(mesh):
    nocc, nvir = mesh.shape["occ"], mesh.shape["vir"]
    return jax.shard_map(
        functools.partial(on_device, nocc, nvir),
        mesh=mesh,
        in_specs=(P("occ", "vir"), P("vir", "occ"), P("occ", "vir")),
        out_specs=P("occ", "vir"),
        check_vma=False,
    )
```

profile of v0, /device:TPU:13, one launch (start us, length us, event | category | flops | bytes accessed | tf_op | source)
XLA Modules:
  0.0 32.7 jit_solution(4243669202297214545)
XLA Ops:
  0.0 31.1 %shard_map.37 = bf16[512,64]{1,0:T(8,128)(2,1)} custom-call(s32[4,16]{1,0:T(4,128)} %active.1, bf16[512,2048]{1,0:T(8,128)(2,1)} %a_hbm.1, bf16[2048,128]{1,0:T(8,128)(2,1)} %b_hbm.1), custom_call_target="tpu_custom_call" | custom-call | tf_op jit(solution)/shard_map/pallas_call | solution.py:293
  31.1 1.6 %copy.4 = bf16[512,64]{0,1:T(8,128)(2,1)} copy(bf16[512,64]{1,0:T(8,128)(2,1)} %shard_map.37) | data formatting | bytes 131072 | tf_op jit(solution)/shard_map/pallas_call | solution.py:293
where the time goes:
time: 32.9 us; the launch traced here: 32.7 us
  Pallas kernels  31.1 us (95%)
  local copies, waits for them, and re-layouts  1.62 us (5%)
    pallas_call x1, Pallas kernels, on_device(): pl.pallas_call(functools.partial(kernel, p, q, nz), out_shape=jax.ShapeDt...  31.1 us
    pallas_call x1, local copies, waits for them, and re-layouts, on_device(): pl.pallas_call(functools.partial(kernel, p, q, nz), out_shape=jax.ShapeDt...  1.62 us

commit v1 on v0

--- a/solution.py
+++ b/solution.py
@@ -266,7 +266,7 @@
                 piece = pltpu.roll(sums[g, k], turn, 1) if turn else sums[g, k]
                 value = piece if value is None else jnp.where(small == g, piece, value)
             start = r * tall + k * short
-            out[start : start + short] = value[:, : width // 2].astype(out.dtype)
+            out[:, start : start + short] = value.T[: width // 2].astype(out.dtype)
 
     for copy in sends:
         copy.wait_send()
@@ -290,9 +290,9 @@
     f32 = jnp.float32
     any_space = pl.BlockSpec(memory_space=pl.ANY)
     dma = pltpu.SemaphoreType.DMA
-    return pl.pallas_call(
+    result = pl.pallas_call(
         functools.partial(kernel, p, q, nz),
-        out_shape=jax.ShapeDtypeStruct((rows, width // 2), jnp.bfloat16),
+        out_shape=pltpu.VMEM((width // 2, rows), jnp.bfloat16),
         in_specs=[pl.BlockSpec(memory_space=pltpu.SMEM), any_space, any_space],
         out_specs=pl.BlockSpec(memory_space=pltpu.VMEM),
         scratch_shapes=[
@@ -308,8 +308,11 @@
             dma((nocc, g)), dma((nocc, g)), dma((nocc, g)), dma((g // 2, nz, 2)),
             pltpu.SemaphoreType.REGULAR((nz - 1, 2)),
         ],
-        compiler_params=pltpu.CompilerParams(collective_id=0, has_side_effects=True),
+        compiler_params=pltpu.CompilerParams(
+            collective_id=0, has_side_effects=True
+        ),
     )(active, amplitudes, integrals)
+    return result.T
 
 
 def solution(mesh):

time: 32.9 us -> 31.7 us (0.964)
  local copies, waits for them, and re-layouts: 1.62 us -> 0.63 us
    pallas_call x1 -> x0, local copies, waits for them, and re-layouts: 1.62 us -> none  [on_device(): pl.pallas_call(functools.partial(kernel, p, q, nz), out_shape=jax.ShapeDt...]
    unnamed x0 -> x1, local copies, waits for them, and re-layouts: none -> 0.63 us
where the time goes in v1:
time: 31.7 us; the launch traced here: 31.5 us
  Pallas kernels  30.9 us (97%)
  local copies, waits for them, and re-layouts  0.63 us (2%)
    pallas_call x1, Pallas kernels, on_device(): pl.pallas_call(functools.partial(kernel, p, q, nz), out_shape=pltpu.VMEM(...  30.9 us

profile of v1, /device:TPU:13, one launch (start us, length us, event | category | flops | bytes accessed | tf_op | source)
XLA Modules:
  0.0 31.5 jit_solution(1208251350058340780)
XLA Ops:
  0.0 30.9 %shard_map.37 = bf16[64,512]{1,0:T(8,128)(2,1)S(1)} custom-call(s32[4,16]{1,0:T(4,128)} %active.1, bf16[512,2048]{1,0:T(8,128)(2,1)} %a_hbm.1, bf16[2048,128]{1,0:T(8,128)(2,1)} %b_hbm.1), custom_call_target="tpu_custom_call" | custom-call | tf_op jit(solution)/shard_map/pallas_call | solution.py:293
  30.9 0.6 %copy.5 = bf16[512,64]{0,1:T(8,128)(2,1)} copy(bf16[512,64]{0,1:T(8,128)(2,1)S(1)} %bitcast.1) | data formatting | bytes 131072

commit v2 on v1

--- a/solution.py
+++ b/solution.py
@@ -21,7 +21,7 @@
 
 
 def kernel(
-    p, q, nz, active, a_hbm, b_hbm, out, a, raw, b, part, got, zsend, zrecv,
+    p, q, nz, active_hbm, a_hbm, b_hbm, out, active, active_sem, a, raw, b, part, got, zsend, zrecv,
     a_sem, b_sem, own_sem, fwd_sem, recv_sem, give_sem, got_sem, zsend_sem, zrecv_sem, reach_sem,
 ):
     o = lax.axis_index("occ")
@@ -51,8 +51,6 @@
 
     b_copy = pltpu.make_async_copy(b_hbm, raw, b_sem)
     b_copy.start()
-    a_copy = pltpu.make_async_copy(a_hbm, a, a_sem)
-    a_copy.start()
 
     barrier = pltpu.get_barrier_semaphore()
     near = [sibling]
@@ -63,13 +61,19 @@
     pl.when(z > 0)(lambda: signal(barrier, below))
     pl.when(z < nz - 1)(lambda: signal(barrier, above))
 
+    a_copy = pltpu.make_async_copy(a_hbm, a, a_sem)
+    a_copy.start()
+    active_copy = pltpu.make_async_copy(active_hbm, active, active_sem)
+    active_copy.start()
+
     def group_of(shape):
         return lax.div(lax.broadcasted_iota(jnp.int32, shape, 1), sub)
 
     b_copy.wait()
     group = group_of((deep, width))
     quarters = [raw[k * deep : (k + 1) * deep].astype(f32) for k in range(CHUNKS)]
-    for j in range(CHUNKS):
+
+    def pack(j):
         packed = None
         for k in range(CHUNKS):
             turn = (sub * (k - j)) % width
@@ -77,6 +81,7 @@
             packed = piece if packed is None else jnp.where(group == k, piece, packed)
         b[0, j] = packed.astype(b.dtype)
 
+    pack(0)
     beside = lax.div(z + nz - 1, nz) + lax.div(2 * nz - 2 - z, nz)
     pl.semaphore_wait(barrier, len(near) + beside)
 
@@ -127,15 +132,19 @@
 
     send_own(0, 0)
     send_own(0, 1)
+    reach(0)
+    pack(1)
     send_own(1, 0)
-    reach(0)
+    for j in range(2, CHUNKS):
+        pack(j)
 
     a_copy.wait()
+    active_copy.wait()
     for r in range(rows // TILE):
         for e in range(depth // TILE):
             place = (pl.ds(r * TILE, TILE), pl.ds(e * TILE, TILE))
             weight = active[r, e].astype(f32)
-            a[place] = (a[place].astype(f32) * weight).astype(a.dtype)
+            a[place] = a[place] * jnp.full((TILE, TILE), weight, f32).astype(a.dtype)
 
     for step in range(1, nz - 1):
         reached(step - 1)
@@ -293,9 +302,10 @@
     result = pl.pallas_call(
         functools.partial(kernel, p, q, nz),
         out_shape=pltpu.VMEM((width // 2, rows), jnp.bfloat16),
-        in_specs=[pl.BlockSpec(memory_space=pltpu.SMEM), any_space, any_space],
+        in_specs=[any_space, any_space, any_space],
         out_specs=pl.BlockSpec(memory_space=pltpu.VMEM),
         scratch_shapes=[
+            pltpu.SMEM(active.shape, active.dtype), dma(()),
             pltpu.VMEM((rows, depth), amplitudes.dtype),
             pltpu.VMEM((depth, width), integrals.dtype),
             pltpu.VMEM((nocc, g, depth // g, width), integrals.dtype),

time: 31.7 us -> 30.7 us (0.968)
  Pallas kernels: 30.9 us -> 29.9 us
    pallas_call x1, Pallas kernels: 30.9 us -> 29.9 us  [on_device(): pl.pallas_call(functools.partial(kernel, p, q, nz), out_shape=pltpu.VMEM(...]
where the time goes in v2:
time: 30.7 us; the launch traced here: 30.5 us
  Pallas kernels  29.9 us (97%)
  local copies, waits for them, and re-layouts  0.63 us (2%)
    pallas_call x1, Pallas kernels, on_device(): pl.pallas_call(functools.partial(kernel, p, q, nz), out_shape=pltpu.VMEM(...  29.9 us
    unnamed x1, local copies, waits for them, and re-layouts  0.63 us

profile of v2, /device:TPU:13, one launch (start us, length us, event | category | flops | bytes accessed | tf_op | source)
XLA Modules:
  0.0 30.5 jit_solution(6286007028427645557)
XLA Ops:
  0.0 29.9 %shard_map.37 = bf16[64,512]{1,0:T(8,128)(2,1)S(1)} custom-call(s32[4,16]{1,0:T(4,128)} %active_hbm.1, bf16[512,2048]{1,0:T(8,128)(2,1)} %a_hbm.1, bf16[2048,128]{1,0:T(8,128)(2,1)} %b_hbm.1), custom_call_target="tpu_custom_call" | custom-call | tf_op jit(solution)/shard_map/pallas_call | solution.py:302
  29.9 0.6 %copy.5 = bf16[512,64]{0,1:T(8,128)(2,1)} copy(bf16[512,64]{0,1:T(8,128)(2,1)S(1)} %bitcast.1) | data formatting | bytes 131072

commit v3 on v2

--- a/solution.py
+++ b/solution.py
@@ -209,7 +209,7 @@
 
     def run(dp, dq, j):
         pending.append(multiply(dp, dq, j))
-        while len(pending) > 1:
+        while len(pending) > 2:
             hand_over(*pending.pop(0))
 
     def diagonals(j):

time: 30.7 us -> 30.8 us (level)
  no operation moved by 1% of the time
where the time goes in v3:
time: 30.8 us; the launch traced here: 30.7 us
  Pallas kernels  30.1 us (98%)
  local copies, waits for them, and re-layouts  0.63 us (2%)
    pallas_call x1, Pallas kernels, on_device(): pl.pallas_call(functools.partial(kernel, p, q, nz), out_shape=pltpu.VMEM(...  30.1 us
    unnamed x1, local copies, waits for them, and re-layouts  0.63 us

profile of v3, /device:TPU:13, one launch (start us, length us, event | category | flops | bytes accessed | tf_op | source)
XLA Modules:
  0.0 30.7 jit_solution(1749667352056253941)
XLA Ops:
  0.0 30.1 %shard_map.37 = bf16[64,512]{1,0:T(8,128)(2,1)S(1)} custom-call(s32[4,16]{1,0:T(4,128)} %active_hbm.1, bf16[512,2048]{1,0:T(8,128)(2,1)} %a_hbm.1, bf16[2048,128]{1,0:T(8,128)(2,1)} %b_hbm.1), custom_call_target="tpu_custom_call" | custom-call | tf_op jit(solution)/shard_map/pallas_call | solution.py:302
  30.1 0.6 %copy.5 = bf16[512,64]{0,1:T(8,128)(2,1)} copy(bf16[512,64]{0,1:T(8,128)(2,1)S(1)} %bitcast.1) | data formatting | bytes 131072
